TPU v7x, 32 devices: a whole 2x2x4 slice. The times are simulated.
32 devices in a mesh: groups: 2 (over x), col: 16 (over z, y, core).
Axes of the slice: x: 2, y: 2, z: 4, core: 2. Of those that a mesh axis runs over, the one named last changes fastest.
Arguments:
- features: bfloat16 [32, 8, 8192], P(('groups', 'col')), parts along dimension 0
- zone_ids: int32 [32], P(('groups', 'col')), parts along dimension 0, may hold values from 0 to 7, as said below
- golden_owner: int32 [16], P('groups'), parts along dimension 0, may hold values from 0 to 15, as said below
- defect_mask: int32 [32, 8, 128], P(('groups', 'col')), parts along dimension 0, may hold values 0 or 1
- kernels: bfloat16 [2, 576, 64], replicated, may hold values from -0.25 to 0.25
Outputs:
- score: float32 [32, 8, 128], P(('groups', 'col')), parts along dimension 0
There are 2 independent parts, one for each index of `groups`. A program takes and returns all parts, laid end to end along the dimension named above; an argument that names none is the same for every part. Nothing has to cross between parts.
Inputs may be any that keep to these rules, and one draw needn't show every extreme that they name: `zone_ids`: every zone holds at least one die. golden_owner[z] is a die of zone z.
All inputs are finite; a program needn't handle non-finite values. No bound on the sum of `defect_mask` on one device may be relied on, other than what follows from the above.
Results may differ from a plain program's by a relative error of at most 0.0039.
Values may be sent and summed in bfloat16 or wider, within the bound.
A program may use at most 64 MiB of HBM per device.

v0:
```python
import jax
import jax.numpy as jnp
from jax import lax
from jax.sharding import PartitionSpec as P

C = 64
SHIFT = 6
BOX = 5
Z = 8


def box_sum(plane):
    rows = plane.shape[0]
    cols = plane.shape[1]
    reach = BOX // 2
    padded = jnp.pad(plane, ((reach, reach), (reach, reach)))
    across = padded[0:rows]
    for offset in range(1, BOX):
        across = across + padded[offset : offset + rows]
    total = across[:, 0:cols]
    for offset in range(1, BOX):
        total = total + across[:, offset : offset + cols]
    return total


def channel_sum(values, chans):
    return jnp.sum(values.reshape(values.shape[0], -1, chans), axis=-1)


def align_golden(test_tile, golden_tile, chans):
    height, spread = test_tile.shape
    width = spread // chans
    side = 2 * SHIFT + 1
    test_f = test_tile.astype(jnp.float32)
    padded = jnp.pad(golden_tile, ((SHIFT, SHIFT), (SHIFT * chans, SHIFT * chans)))
    padded_f = padded.astype(jnp.float32)
    golden_sq = channel_sum(padded_f * padded_f, chans)
    self_energy = box_sum(channel_sum(test_f * test_f, chans))

    def row_step(carry, row_off):
        numer, denom = carry
        band = lax.dynamic_slice_in_dim(padded, row_off, height, 0).astype(jnp.float32)
        sq_band = lax.dynamic_slice_in_dim(golden_sq, row_off, height, 0)
        for col_off in range(side):
            moved = band[:, col_off * chans : col_off * chans + spread]
            cross = box_sum(channel_sum(test_f * moved, chans))
            other = box_sum(sq_band[:, col_off : col_off + width])
            expo = jnp.exp(32.0 * cross / jnp.sqrt(self_energy * other + 1e-05))
            numer = numer + jnp.repeat(expo, chans, axis=1) * moved
            denom = denom + expo
        return ((numer, denom), None)

    start = (jnp.zeros((height, spread), jnp.float32), jnp.zeros((height, width), jnp.float32))
    (numer, denom), _ = lax.scan(row_step, start, jnp.arange(side, dtype=jnp.int32))
    return numer / jnp.repeat(denom, chans, axis=1)


def conv_three(tile, kernel):
    height, width, chans = tile.shape
    padded = jnp.pad(tile, ((1, 1), (1, 1), (0, 0)))
    windows = []
    for tap in range(9):
        row_off = tap // 3
        col_off = tap % 3
        windows.append(
            padded[row_off : row_off + height, col_off : col_off + width].reshape(
                height * width, chans
            )
        )
    stacked = jnp.concatenate(windows, axis=1)
    total = jnp.dot(stacked, kernel, preferred_element_type=jnp.float32)
    return total.reshape(height, width, kernel.shape[1])


def body(features, zone_ids, golden_owner, defect_mask, kernels):
    height = features.shape[1]
    width = defect_mask.shape[2]
    my_zone = zone_ids[0]
    wanted = golden_owner[my_zone]
    piece = lax.all_gather(features, "col", axis=0, tiled=True)
    positions = jnp.arange(piece.shape[0], dtype=jnp.int32)
    chosen = jnp.where((positions == wanted)[:, None, None], piece, jnp.zeros_like(piece))
    golden = jnp.sum(chosen, axis=0, keepdims=True)
    test_tile = features[0]
    aligned = align_golden(test_tile, golden[0], C)
    residual = (
        (test_tile.astype(jnp.float32) - aligned).astype(jnp.bfloat16).reshape(height, width, C)
    )
    hidden = jax.nn.relu(conv_three(residual, kernels[0])).astype(jnp.bfloat16)
    refined = residual.astype(jnp.float32) + conv_three(hidden, kernels[1])
    energy = jnp.mean(refined * refined, axis=-1)
    masked = defect_mask[0].astype(jnp.float32)
    die_sum = jnp.sum(energy * masked)
    die_count = jnp.sum(masked)
    onehot = (jnp.arange(Z, dtype=jnp.int32) == my_zone).astype(jnp.float32)
    zone_sum, zone_count = lax.psum((onehot * die_sum, onehot * die_count), "col")
    zone_mean = zone_sum / jnp.maximum(zone_count, 1.0)
    mine = jnp.sum(onehot * zone_mean)
    return (energy / (mine + 0.01))[None]


def solution(mesh):
    in_specs = (
        P(("groups", "col"), None, None),
        P(("groups", "col")),
        P("groups"),
        P(("groups", "col"), None, None),
        P(),
    )
    out_specs = P(("groups", "col"), None, None)
    return jax.shard_map(body, mesh=mesh, in_specs=in_specs, out_specs=out_specs, check_vma=False)
```

profile of v0, /device:TPU:0, one launch (start us, length us, event | category | flops | bytes accessed | tf_op | source)
XLA Modules:
  0.0 422.0 jit_solution(12637861433031280978)
XLA Ops:
  11.4 42.3 %all-gather.2.cloned.1.call-done = bf16[16,8,8192]{2,1,0:T(8,128)(2,1)} async-done(((bf16[1,8,8192]{2,1,0:T(8,128)(2,1)}), bf16[16,8,8192]{2,1,0:T(8,128)(2,1)}) %all-gather.2.cloned.1.call-update) | async-done | bytes 2097168 | tf_op jit(solution)/shard_map/all_gather | solution.py:80
  53.7 2.0 select_reduce_fusion
  57.7 318.3 %while.15 = (s32[]{:T(128)}, f32[8,8192]{1,0:T(8,128)}, f32[8,128]{1,0:T(8,128)S(1)}, s32[13]{0:T(128)S(1)}, bf16[20,8960]{1,0:T(8,128)(2,1)}, /*index=5*/f32[8,...) while((s32[]{:T(128)}, f32[8,8192]{1,0:T(8,128)}, ...), condition=%wide.region_17.18_spmd.clone, body=%wide.region_3.17_spmd.clone.sunk | while | flops 3815698 | bytes 38420288 | solution.py:54
  61.1 1.3 slice_multiply_fusion.14
  79.7 2.4 fusion.283
  85.5 1.3 slice_multiply_fusion.14
  104.1 2.5 fusion.283
  110.0 1.3 slice_multiply_fusion.14
  128.6 2.5 fusion.283
  134.5 1.3 slice_multiply_fusion.14
  153.1 2.5 fusion.283
  159.0 1.3 slice_multiply_fusion.14
  177.6 2.5 fusion.283
  183.4 1.3 slice_multiply_fusion.14
  202.1 2.5 fusion.283
  207.9 1.3 slice_multiply_fusion.14
  226.6 2.5 fusion.283
  232.4 1.3 slice_multiply_fusion.14
  251.1 2.5 fusion.283
  256.9 1.3 slice_multiply_fusion.14
  275.6 2.5 fusion.283
  281.4 1.3 slice_multiply_fusion.14
  300.1 2.5 fusion.283
  305.9 1.3 slice_multiply_fusion.14
  324.5 2.5 fusion.283
  330.4 1.3 slice_multiply_fusion.14
  333.1 1.1 reshape.318
  349.0 2.5 fusion.283
  354.9 1.3 slice_multiply_fusion.14
  373.5 2.5 fusion.283
  380.5 1.3 fusion.234
  381.8 31.4 %all-reduce.30 = (f32[8]{0:T(128)S(1)}, f32[8]{0:T(128)S(1)}) all-reduce(f32[8]{0:T(128)S(1)} %get-tuple-element.221, f32[8]{0:T(128)S(1)} %get-tuple-element.220), channel_id=1, replica_groups=mesh['groups'=2,'col'=16] {'col'}, use_global_device_ids=true, to_apply=%region_20.21 | all-reduce | flops 16 | bytes 128 | tf_op jit(solution)/shard_map/psum | solution.py:96
  (1006 shorter events, 251.4 us)
Async XLA Ops:
  6.5 4.8 %copy-start.3 = (bf16[1,8,8192]{2,1,0:T(8,128)(2,1)S(1)}, bf16[1,8,8192]{2,1,0:T(8,128)(2,1)}, u32[]{:S(2)}) copy-start(bf16[1,8,8192]{2,1,0:T(8,128)(2,1)} %param.7) | copy-start | bytes 393220
  6.5 2.6 copy-start.7
  6.5 4.0 copy-start.6
  6.5 47.1 %all-gather.2.cloned.1.call-start = ((), (), s32[]{:S(2)}) async-start(), calls=%async_computation | async-start | bytes 2228224 | tf_op jit(solution)/shard_map/all_gather | solution.py:80
  57.7 4.7 %copy-start = (f32[8,8192]{1,0:T(8,128)}, f32[8,8192]{1,0:T(8,128)S(1)}, u32[]{:S(2)}) copy-start(f32[8,8192]{1,0:T(8,128)S(1)} %get-tuple-element.456) | copy-start | bytes 786436 | tf_op jit(solution)/shard_map/while
  79.7 2.4 copy-start.1
  82.1 4.7 %copy-start = (f32[8,8192]{1,0:T(8,128)}, f32[8,8192]{1,0:T(8,128)S(1)}, u32[]{:S(2)}) copy-start(f32[8,8192]{1,0:T(8,128)S(1)} %get-tuple-element.456) | copy-start | bytes 786436 | tf_op jit(solution)/shard_map/while
  104.1 2.5 copy-start.1
  106.6 4.7 %copy-start = (f32[8,8192]{1,0:T(8,128)}, f32[8,8192]{1,0:T(8,128)S(1)}, u32[]{:S(2)}) copy-start(f32[8,8192]{1,0:T(8,128)S(1)} %get-tuple-element.456) | copy-start | bytes 786436 | tf_op jit(solution)/shard_map/while
  128.6 2.5 copy-start.1
  131.1 4.7 %copy-start = (f32[8,8192]{1,0:T(8,128)}, f32[8,8192]{1,0:T(8,128)S(1)}, u32[]{:S(2)}) copy-start(f32[8,8192]{1,0:T(8,128)S(1)} %get-tuple-element.456) | copy-start | bytes 786436 | tf_op jit(solution)/shard_map/while
  153.1 2.5 copy-start.1
  155.6 4.7 %copy-start = (f32[8,8192]{1,0:T(8,128)}, f32[8,8192]{1,0:T(8,128)S(1)}, u32[]{:S(2)}) copy-start(f32[8,8192]{1,0:T(8,128)S(1)} %get-tuple-element.456) | copy-start | bytes 786436 | tf_op jit(solution)/shard_map/while
  177.6 2.5 copy-start.1
  180.1 4.7 %copy-start = (f32[8,8192]{1,0:T(8,128)}, f32[8,8192]{1,0:T(8,128)S(1)}, u32[]{:S(2)}) copy-start(f32[8,8192]{1,0:T(8,128)S(1)} %get-tuple-element.456) | copy-start | bytes 786436 | tf_op jit(solution)/shard_map/while
  202.1 2.5 copy-start.1
  204.6 4.7 %copy-start = (f32[8,8192]{1,0:T(8,128)}, f32[8,8192]{1,0:T(8,128)S(1)}, u32[]{:S(2)}) copy-start(f32[8,8192]{1,0:T(8,128)S(1)} %get-tuple-element.456) | copy-start | bytes 786436 | tf_op jit(solution)/shard_map/while
  226.6 2.5 copy-start.1
  229.1 4.7 %copy-start = (f32[8,8192]{1,0:T(8,128)}, f32[8,8192]{1,0:T(8,128)S(1)}, u32[]{:S(2)}) copy-start(f32[8,8192]{1,0:T(8,128)S(1)} %get-tuple-element.456) | copy-start | bytes 786436 | tf_op jit(solution)/shard_map/while
  251.1 2.5 copy-start.1
  253.6 4.7 %copy-start = (f32[8,8192]{1,0:T(8,128)}, f32[8,8192]{1,0:T(8,128)S(1)}, u32[]{:S(2)}) copy-start(f32[8,8192]{1,0:T(8,128)S(1)} %get-tuple-element.456) | copy-start | bytes 786436 | tf_op jit(solution)/shard_map/while
  275.6 2.5 copy-start.1
  278.1 4.7 %copy-start = (f32[8,8192]{1,0:T(8,128)}, f32[8,8192]{1,0:T(8,128)S(1)}, u32[]{:S(2)}) copy-start(f32[8,8192]{1,0:T(8,128)S(1)} %get-tuple-element.456) | copy-start | bytes 786436 | tf_op jit(solution)/shard_map/while
  300.1 2.5 copy-start.1
  302.6 4.7 %copy-start = (f32[8,8192]{1,0:T(8,128)}, f32[8,8192]{1,0:T(8,128)S(1)}, u32[]{:S(2)}) copy-start(f32[8,8192]{1,0:T(8,128)S(1)} %get-tuple-element.456) | copy-start | bytes 786436 | tf_op jit(solution)/shard_map/while
  324.5 2.5 copy-start.1
  327.1 4.7 %copy-start = (f32[8,8192]{1,0:T(8,128)}, f32[8,8192]{1,0:T(8,128)S(1)}, u32[]{:S(2)}) copy-start(f32[8,8192]{1,0:T(8,128)S(1)} %get-tuple-element.456) | copy-start | bytes 786436 | tf_op jit(solution)/shard_map/while
  349.0 2.5 copy-start.1
  351.6 4.7 %copy-start = (f32[8,8192]{1,0:T(8,128)}, f32[8,8192]{1,0:T(8,128)S(1)}, u32[]{:S(2)}) copy-start(f32[8,8192]{1,0:T(8,128)S(1)} %get-tuple-element.456) | copy-start | bytes 786436 | tf_op jit(solution)/shard_map/while
  373.5 2.5 copy-start.1
  376.0 1.0 copy-start.2
  376.0 1.0 copy-start.4
  (1 other events, 0.9 us)
Sparse Core Ops, SparseCore 0:
  9.5 44.0 all-gather.1
where the time goes:
time: 425 us; the launch traced here: 422 us
  local copies, waits for them, and re-layouts  179 us (42%)
  other arithmetic  125 us (29%)
  waiting for transfers between devices  43 us (10%)
  blocking collectives  31.4 us (7%)
  loops' own time  27.6 us (6%)
  between operations  15 us (4%)
    reshape x170, local copies, waits for them, and re-layouts, channel_sum(): return jnp.sum(values.reshape(values.shape[0], -1, chans), axis=-1)  73.2 us
    reshape x169, local copies, waits for them, and re-layouts, row_step(): numer = numer + jnp.repeat(expo, chans, axis=1) * moved  59 us
    all_gather x1, waiting for transfers between devices, body(): piece = lax.all_gather(features, 'col', axis=0, tiled=True)  42.3 us
    reduce_sum x171, other arithmetic, channel_sum(): return jnp.sum(values.reshape(values.shape[0], -1, chans), axis=-1)  35.9 us
    add x13, other arithmetic, row_step(): numer = numer + jnp.repeat(expo, chans, axis=1) * moved  32.5 us
    broadcast_in_dim x169, local copies, waits for them, and re-layouts, row_step(): numer = numer + jnp.repeat(expo, chans, axis=1) * moved  32.3 us
    psum x1, blocking collectives, body(): lax.psum((onehot * die_sum, onehot * die_count), 'col')  31.4 us
    another operation x1, loops' own time, align_golden(): lax.scan(row_step, start, jnp.arange(side, dtype=jnp.int32))  27.6 us
  transfers between devices with their start and end apart: 1, of which 1 were waited for; matrix products, arithmetic and copies ran while one was open for 1% of the time, Pallas kernels for 0%

commit v1 on v0

--- a/solution.py
+++ b/solution.py
@@ -77,7 +77,16 @@
     width = defect_mask.shape[2]
     my_zone = zone_ids[0]
     wanted = golden_owner[my_zone]
-    piece = lax.all_gather(features, "col", axis=0, tiled=True)
+    last, row_out = (lax.axis_size("col"), lax.axis_index("col"))
+    piece, before = (features, 1)
+    while before < last:
+        parts_out = lax.ppermute(
+            piece, axis_name="col", perm=[(dev_j, dev_j ^ before) for dev_j in range(last)]
+        )
+        x_new = jnp.concatenate([piece, parts_out], axis=0)
+        upper = jnp.concatenate([parts_out, piece], 0)
+        piece = jnp.where(row_out & before == 0, x_new, upper)
+        before = 2 * before
     positions = jnp.arange(piece.shape[0], dtype=jnp.int32)
     chosen = jnp.where((positions == wanted)[:, None, None], piece, jnp.zeros_like(piece))
     golden = jnp.sum(chosen, axis=0, keepdims=True)

time: 425 us -> 440 us (1.035)
  waiting for transfers between devices: 43 us -> 59.9 us
  between operations: 15 us -> 1.62 us
  starting transfers between devices: 0.01 us -> 7.81 us
    ppermute x0 -> x4, waiting for transfers between devices: none -> 59.9 us  [body(): lax.ppermute(piece, axis_name='col', perm=[(dev_j, dev_j ^ before) for de...]
    all_gather x1 -> x0, waiting for transfers between devices: 42.3 us -> none  [body(): piece = lax.all_gather(features, 'col', axis=0, tiled=True)]
    ppermute x0 -> x4, starting transfers between devices: none -> 7.81 us  [body(): lax.ppermute(piece, axis_name='col', perm=[(dev_j, dev_j ^ before) for de...]
  transfers between devices with their start and end apart: 1 -> 4, of which waited for: 1 -> 4; matrix products, arithmetic and copies ran while one was open for 1% -> 1% of each run, Pallas kernels for 0% -> 0%
where the time goes in v1:
time: 440 us; the launch traced here: 438 us
  local copies, waits for them, and re-layouts  180 us (41%)
  other arithmetic  125 us (28%)
  waiting for transfers between devices  59.9 us (14%)
  blocking collectives  33.1 us (8%)
  loops' own time  30 us (7%)
  starting transfers between devices  7.81 us (2%)
    reshape x170, local copies, waits for them, and re-layouts, channel_sum(): return jnp.sum(values.reshape(values.shape[0], -1, chans), axis=-1)  73.2 us
    ppermute x4, waiting for transfers between devices, body(): lax.ppermute(piece, axis_name='col', perm=[(dev_j, dev_j ^ before) for de...  59.9 us
    reshape x169, local copies, waits for them, and re-layouts, row_step(): numer = numer + jnp.repeat(expo, chans, axis=1) * moved  59.2 us
    reduce_sum x171, other arithmetic, channel_sum(): return jnp.sum(values.reshape(values.shape[0], -1, chans), axis=-1)  35.9 us
    psum x1, blocking collectives, body(): lax.psum((onehot * die_sum, onehot * die_count), 'col')  33.1 us
    broadcast_in_dim x169, local copies, waits for them, and re-layouts, row_step(): numer = numer + jnp.repeat(expo, chans, axis=1) * moved  32.3 us
    add x13, other arithmetic, row_step(): numer = numer + jnp.repeat(expo, chans, axis=1) * moved  32.1 us
    another operation x1, loops' own time, align_golden(): lax.scan(row_step, start, jnp.arange(side, dtype=jnp.int32))  30 us
  transfers between devices with their start and end apart: 4, of which 4 were waited for; matrix products, arithmetic and copies ran while one was open for 1% of the time, Pallas kernels for 0%

profile of v1, /device:TPU:0, one launch (start us, length us, event | category | flops | bytes accessed | tf_op | source)
XLA Modules:
  0.0 437.9 jit_solution(10875953348137278870)
XLA Ops:
  2.7 2.9 collective-permute-start.1
  8.3 3.9 collective-permute-done.1
  12.3 1.9 collective-permute-start.2
  15.7 10.2 %collective-permute-done.2 = bf16[4,8,8192]{2,1,0:T(8,128)(2,1)S(1)} collective-permute-done((bf16[4,8,8192]{2,1,0:T(8,128)(2,1)S(1)}, bf16[4,8,8192]{2,1,0:T(8,128)(2,1)S(1)}, u32[]{:S(2)}, u32[]{:S(2)}) %collective-permute-start.2) | collective-permute-done | bytes 524320 | tf_op jit(solution)/shard_map/ppermute | solution.py:83
  26.0 2.6 collective-permute-start.3
  28.6 44.7 %collective-permute-done.3 = bf16[8,8,8192]{2,1,0:T(8,128)(2,1)S(1)} collective-permute-done((bf16[8,8,8192]{2,1,0:T(8,128)(2,1)S(1)}, bf16[8,8,8192]{2,1,0:T(8,128)(2,1)S(1)}, u32[]{:S(2)}, u32[]{:S(2)}) %collective-permute-start.3) | collective-permute-done | bytes 1048608 | tf_op jit(solution)/shard_map/ppermute | solution.py:83
  76.1 321.0 %while.15 = (s32[]{:T(128)}, f32[8,8192]{1,0:T(8,128)}, f32[8,128]{1,0:T(8,128)S(1)}, s32[13]{0:T(128)S(1)}, bf16[20,8960]{1,0:T(8,128)(2,1)}, /*index=5*/f32[8,...) while((s32[]{:T(128)}, f32[8,8192]{1,0:T(8,128)}, ...), condition=%wide.region_17.18_spmd.clone, body=%wide.region_3.17_spmd.clone.sunk | while | flops 3815698 | bytes 38420288 | solution.py:54
  79.7 1.3 slice_multiply_fusion.14
  98.4 2.4 fusion.285
  104.3 1.3 slice_multiply_fusion.14
  123.0 2.5 fusion.285
  129.0 1.3 slice_multiply_fusion.14
  147.7 2.5 fusion.285
  153.7 1.3 slice_multiply_fusion.14
  172.4 2.5 fusion.285
  178.4 1.3 slice_multiply_fusion.14
  197.1 2.5 fusion.285
  203.1 1.3 slice_multiply_fusion.14
  221.8 2.5 fusion.285
  227.8 1.3 slice_multiply_fusion.14
  246.4 2.5 fusion.285
  252.5 1.3 slice_multiply_fusion.14
  271.1 2.5 fusion.285
  277.2 1.3 slice_multiply_fusion.14
  295.8 2.5 fusion.285
  301.9 1.3 slice_multiply_fusion.14
  320.5 2.5 fusion.285
  326.6 1.3 slice_multiply_fusion.14
  345.2 2.5 fusion.285
  369.9 2.5 fusion.285
  394.6 2.5 fusion.285
  402.9 33.1 %all-reduce.30 = (f32[8]{0:T(128)S(1)}, f32[8]{0:T(128)S(1)}) all-reduce(f32[8]{0:T(128)S(1)} %get-tuple-element.221, f32[8]{0:T(128)S(1)} %get-tuple-element.220), channel_id=1, replica_groups=mesh['groups'=2,'col'=16] {'col'}, use_global_device_ids=true, to_apply=%region_20.21 | all-reduce | flops 16 | bytes 128 | tf_op jit(solution)/shard_map/psum | solution.py:105
  (1014 shorter events, 260.1 us)
Async XLA Ops:
  0.0 7.5 %copy-start.7 = (s32[8]{0:T(128)S(1)}, s32[8]{0:T(128)}, u32[]{:S(2)}) copy-start(s32[8]{0:T(128)} %param.9) | copy-start | bytes 100
  0.0 1.6 collective-permute-start
  2.7 9.6 %collective-permute-start.1 = (bf16[2,8,8192]{2,1,0:T(8,128)(2,1)S(1)}, bf16[2,8,8192]{2,1,0:T(8,128)(2,1)S(1)}, u32[]{:S(2)}, u32[]{:S(2)}) collective-permute-start(bf16[2,8,8192]{2,1,0:T(8,128)(2,1)S(1)} %maximum_select_fusion.3), channel_id=1, source_target_pairs={{0,2},{1,3},{2,0},{3,1},{4,6},{5,7},{6,4},{7,5},{8,10},{9,11},{10,... | collective-permute-start | bytes 786440 | tf_op jit(solution)/shard_map/ppermute | solution.py:83
  7.2 7.7 %copy-start.6 = (s32[1,8,128]{2,1,0:T(8,128)S(1)}, s32[1,8,128]{2,1,0:T(8,128)}, u32[]{:S(2)}) copy-start(s32[1,8,128]{2,1,0:T(8,128)} %param.10) | copy-start | bytes 12292
  12.3 16.3 %copy-start.3 = (bf16[1,8,8192]{2,1,0:T(8,128)(2,1)S(1)}, bf16[1,8,8192]{2,1,0:T(8,128)(2,1)}, u32[]{:S(2)}) copy-start(bf16[1,8,8192]{2,1,0:T(8,128)(2,1)} %param.7) | copy-start | bytes 393220
  12.3 13.5 %collective-permute-start.2 = (bf16[4,8,8192]{2,1,0:T(8,128)(2,1)S(1)}, bf16[4,8,8192]{2,1,0:T(8,128)(2,1)S(1)}, u32[]{:S(2)}, u32[]{:S(2)}) collective-permute-start(bf16[4,8,8192]{2,1,0:T(8,128)(2,1)S(1)} %maximum_select_fusion.2), channel_id=1, source_target_pairs={{0,4},{1,5},{2,6},{3,7},{4,0},{5,1},{6,2},{7,3},{8,12},{9,13},{10,... | collective-permute-start | bytes 1572872 | tf_op jit(solution)/shard_map/ppermute | solution.py:83
  26.0 47.2 %collective-permute-start.3 = (bf16[8,8,8192]{2,1,0:T(8,128)(2,1)S(1)}, bf16[8,8,8192]{2,1,0:T(8,128)(2,1)S(1)}, u32[]{:S(2)}, u32[]{:S(2)}) collective-permute-start(bf16[8,8,8192]{2,1,0:T(8,128)(2,1)S(1)} %maximum_select_fusion.1), channel_id=1, source_target_pairs={{0,8},{1,9},{2,10},{3,11},{4,12},{5,13},{6,14},{7,15},{8,0},{9,1},... | collective-permute-start | bytes 3145736 | tf_op jit(solution)/shard_map/ppermute | solution.py:83
  76.1 4.9 %copy-start = (f32[8,8192]{1,0:T(8,128)}, f32[8,8192]{1,0:T(8,128)S(1)}, u32[]{:S(2)}) copy-start(f32[8,8192]{1,0:T(8,128)S(1)} %get-tuple-element.456) | copy-start | bytes 786436 | tf_op jit(solution)/shard_map/while
  100.8 4.9 %copy-start = (f32[8,8192]{1,0:T(8,128)}, f32[8,8192]{1,0:T(8,128)S(1)}, u32[]{:S(2)}) copy-start(f32[8,8192]{1,0:T(8,128)S(1)} %get-tuple-element.456) | copy-start | bytes 786436 | tf_op jit(solution)/shard_map/while
  123.0 2.5 copy-start.1
  125.4 4.9 %copy-start = (f32[8,8192]{1,0:T(8,128)}, f32[8,8192]{1,0:T(8,128)S(1)}, u32[]{:S(2)}) copy-start(f32[8,8192]{1,0:T(8,128)S(1)} %get-tuple-element.456) | copy-start | bytes 786436 | tf_op jit(solution)/shard_map/while
  147.7 2.5 copy-start.1
  150.1 4.9 %copy-start = (f32[8,8192]{1,0:T(8,128)}, f32[8,8192]{1,0:T(8,128)S(1)}, u32[]{:S(2)}) copy-start(f32[8,8192]{1,0:T(8,128)S(1)} %get-tuple-element.456) | copy-start | bytes 786436 | tf_op jit(solution)/shard_map/while
  172.4 2.5 copy-start.1
  174.8 4.9 %copy-start = (f32[8,8192]{1,0:T(8,128)}, f32[8,8192]{1,0:T(8,128)S(1)}, u32[]{:S(2)}) copy-start(f32[8,8192]{1,0:T(8,128)S(1)} %get-tuple-element.456) | copy-start | bytes 786436 | tf_op jit(solution)/shard_map/while
  197.1 2.5 copy-start.1
  199.5 4.9 %copy-start = (f32[8,8192]{1,0:T(8,128)}, f32[8,8192]{1,0:T(8,128)S(1)}, u32[]{:S(2)}) copy-start(f32[8,8192]{1,0:T(8,128)S(1)} %get-tuple-element.456) | copy-start | bytes 786436 | tf_op jit(solution)/shard_map/while
  221.8 2.5 copy-start.1
  224.2 4.9 %copy-start = (f32[8,8192]{1,0:T(8,128)}, f32[8,8192]{1,0:T(8,128)S(1)}, u32[]{:S(2)}) copy-start(f32[8,8192]{1,0:T(8,128)S(1)} %get-tuple-element.456) | copy-start | bytes 786436 | tf_op jit(solution)/shard_map/while
  246.4 2.5 copy-start.1
  248.9 4.9 %copy-start = (f32[8,8192]{1,0:T(8,128)}, f32[8,8192]{1,0:T(8,128)S(1)}, u32[]{:S(2)}) copy-start(f32[8,8192]{1,0:T(8,128)S(1)} %get-tuple-element.456) | copy-start | bytes 786436 | tf_op jit(solution)/shard_map/while
  271.1 2.5 copy-start.1
  273.6 4.9 %copy-start = (f32[8,8192]{1,0:T(8,128)}, f32[8,8192]{1,0:T(8,128)S(1)}, u32[]{:S(2)}) copy-start(f32[8,8192]{1,0:T(8,128)S(1)} %get-tuple-element.456) | copy-start | bytes 786436 | tf_op jit(solution)/shard_map/while
  295.8 2.5 copy-start.1
  298.3 4.9 %copy-start = (f32[8,8192]{1,0:T(8,128)}, f32[8,8192]{1,0:T(8,128)S(1)}, u32[]{:S(2)}) copy-start(f32[8,8192]{1,0:T(8,128)S(1)} %get-tuple-element.456) | copy-start | bytes 786436 | tf_op jit(solution)/shard_map/while
  320.5 2.5 copy-start.1
  323.0 4.9 %copy-start = (f32[8,8192]{1,0:T(8,128)}, f32[8,8192]{1,0:T(8,128)S(1)}, u32[]{:S(2)}) copy-start(f32[8,8192]{1,0:T(8,128)S(1)} %get-tuple-element.456) | copy-start | bytes 786436 | tf_op jit(solution)/shard_map/while
  345.2 2.5 copy-start.1
  347.7 4.9 %copy-start = (f32[8,8192]{1,0:T(8,128)}, f32[8,8192]{1,0:T(8,128)S(1)}, u32[]{:S(2)}) copy-start(f32[8,8192]{1,0:T(8,128)S(1)} %get-tuple-element.456) | copy-start | bytes 786436 | tf_op jit(solution)/shard_map/while
  369.9 2.5 copy-start.1
  372.4 4.9 %copy-start = (f32[8,8192]{1,0:T(8,128)}, f32[8,8192]{1,0:T(8,128)S(1)}, u32[]{:S(2)}) copy-start(f32[8,8192]{1,0:T(8,128)S(1)} %get-tuple-element.456) | copy-start | bytes 786436 | tf_op jit(solution)/shard_map/while
  394.6 2.5 copy-start.1
  (4 other events, 5.3 us)
